TPU v7x, 32 devices: a whole 2x2x4 slice. The times are simulated.
32 devices in a mesh: groups: 2 (over y), seq: 16 (over z, x, core).
Axes of the slice: x: 2, y: 2, z: 4, core: 2. Of those that a mesh axis runs over, the one named last changes fastest.
Arguments:
- query_rows: bfloat16 [8192, 8, 128], P(('groups', 'seq')), parts along dimension 0, may hold values from -48 to 48
- key_rows: bfloat16 [8192, 8, 128], P(('groups', 'seq')), parts along dimension 0, may hold values from -7 to 7
- value_rows: bfloat16 [8192, 8, 128], P(('groups', 'seq')), parts along dimension 0, may hold values from -6 to 6
- out_grad: bfloat16 [8192, 8, 128], P(('groups', 'seq')), parts along dimension 0, may hold values from -6 to 6
Outputs:
- attended: bfloat16 [8192, 8, 128], P(('groups', 'seq')), parts along dimension 0
- query_grad: bfloat16 [8192, 8, 128], P(('groups', 'seq')), parts along dimension 0
- key_grad: bfloat16 [8192, 8, 128], P(('groups', 'seq')), parts along dimension 0
- value_grad: bfloat16 [8192, 8, 128], P(('groups', 'seq')), parts along dimension 0
There are 2 independent parts, one for each index of `groups`. A program takes and returns all parts, laid end to end along the dimension named above; each array names one. Nothing has to cross between parts.
All inputs are finite; a program needn't handle non-finite values.
Results may differ from a plain program's by a relative error of at most 0.018.
Values may be sent and summed in bfloat16 or wider, within the bound.
A program may use at most 128 MiB of HBM per device.

v0:
```python
from functools import partial

import jax
import jax.numpy as jnp
from jax import lax
from jax.sharding import PartitionSpec as P

BLOCK = 128


def partner_2(array, axis, stride):
    return lax.ppermute(array, axis, [(i, i ^ 1 << stride) for i in range(lax.axis_size(axis))])


def keep_round(values):
    frozen = lax.stop_gradient(values)
    lowered = lax.optimization_barrier(frozen.astype(jnp.bfloat16))
    return values + (lowered.astype(values.dtype) - frozen)


def coarsen(fields, height):
    row_count = fields.shape[0] >> height
    grouped = fields.reshape((row_count, 1 << height) + fields.shape[1:])
    return keep_round(jnp.mean(grouped, axis=1))


def coarsen_heads(fields, height):
    if height == 0:
        return fields
    row_count = fields.shape[1] >> height
    grouped = fields.reshape((fields.shape[0], row_count, 1 << height, fields.shape[2]))
    return keep_round(jnp.mean(grouped, axis=2))


def to_heads(fields):
    return jnp.transpose(fields, (1, 0, 2))


def block_term(weight, query_blocks, key_blocks, value_blocks):
    factor = query_blocks.shape[-1] ** (-0.5)
    scores = (
        jnp.einsum(
            "hbqd,hbkd->hbqk",
            query_blocks,
            key_blocks,
            precision=lax.Precision.DEFAULT,
            preferred_element_type=jnp.float32,
        )
        * factor
    )
    row_max = lax.stop_gradient(jnp.max(scores, axis=-1))
    weights = jnp.exp(scores - row_max[..., None])
    denominator = weight * jnp.sum(weights, axis=-1)
    numerator = weight * jnp.einsum(
        "hbqk,hbkd->hbqd",
        keep_round(weights),
        value_blocks,
        precision=lax.Precision.DEFAULT,
        preferred_element_type=jnp.float32,
    )
    head_count = query_blocks.shape[0]
    row_count = query_blocks.shape[1] * query_blocks.shape[2]
    return (
        row_max.reshape((head_count, row_count)),
        denominator.reshape((head_count, row_count)),
        numerator.reshape((head_count, row_count, numerator.shape[-1])),
    )


def combine(earlier, second):
    row_max = jnp.maximum(earlier[0], second[0])
    scale_a = jnp.exp(earlier[0] - row_max)
    scale_b = jnp.exp(second[0] - row_max)
    return (
        row_max,
        scale_a * earlier[1] + scale_b * second[1],
        scale_a[..., None] * earlier[2] + scale_b[..., None] * second[2],
    )


def upsample(summary):
    return tuple((jnp.repeat(entry, 2, axis=1) for entry in summary))


def flip_pairs(blocks):
    shaped = blocks.shape
    paired = blocks.reshape((shaped[0], shaped[1] // 2, 2) + shaped[2:])
    return paired[:, :, ::-1].reshape(shaped)


def join_halves(own_part, partner, position, bit_index):
    lower = position >> bit_index & 1 == 0
    return jnp.where(
        lower, jnp.concatenate([own_part, partner], 0), jnp.concatenate([partner, own_part], 0)
    )


def split_halves(cotangent, position, bit_index):
    half_rows = cotangent.shape[0] // 2
    upper_half = position >> bit_index & 1
    own_part = lax.dynamic_slice_in_dim(cotangent, upper_half * half_rows, half_rows, 0)
    partner = lax.dynamic_slice_in_dim(cotangent, (1 - upper_half) * half_rows, half_rows, 0)
    return (own_part, partner)


def fetch_sibling(own_piece, partner_bit, position):
    assembled = partner_2(own_piece, "seq", partner_bit)
    for bit_index in range(partner_bit):
        arrived = partner_2(assembled, "seq", bit_index)
        assembled = join_halves(assembled, arrived, position, bit_index)
    return assembled


def return_sibling(cotangent, partner_bit, position):
    for bit_index in reversed(range(partner_bit)):
        own_part, partner = split_halves(cotangent, position, bit_index)
        cotangent = own_part + partner_2(partner, "seq", bit_index)
    return partner_2(cotangent, "seq", partner_bit)


def on_device(query_rows, key_rows, value_rows, out_grad):
    local_rows = query_rows.shape[0]
    devices = lax.axis_size("seq")
    position = lax.axis_index("seq")
    levels = (local_rows * devices // BLOCK).bit_length() - 1
    remote = [height for height in range(levels) if local_rows >> height < 2 * BLOCK]
    partner_bits = {height: ((BLOCK << height) // local_rows).bit_length() - 1 for height in remote}

    def own_pieces(key32, value32):
        return {
            height: jnp.stack([coarsen(key32, height), coarsen(value32, height)], axis=1)
            for height in remote
        }

    def local_attention(query_flat, key_flat, value_flat, blocks):
        query32 = to_heads(query_flat)
        key32 = to_heads(key_flat)
        value32 = to_heads(value_flat)
        head_count = query32.shape[0]
        width = query32.shape[2]
        summary = None
        for height in reversed(range(levels)):
            query_c = coarsen_heads(query32, height)
            if height in blocks:
                sibling = blocks[height]
                keys_c = to_heads(sibling[:, 0])[:, None]
                values_c = to_heads(sibling[:, 1])[:, None]
                partial_term = block_term(float(1 << height), query_c[:, None], keys_c, values_c)
            else:
                nblocks = query_c.shape[1] // BLOCK
                block_shape = (head_count, nblocks, BLOCK, width)
                keys_c = flip_pairs(coarsen_heads(key32, height).reshape(block_shape))
                values_c = flip_pairs(coarsen_heads(value32, height).reshape(block_shape))
                partial_term = jax.checkpoint(partial(block_term, float(1 << height)))(
                    query_c.reshape(block_shape), keys_c, values_c
                )
            summary = partial_term if summary is None else combine(upsample(summary), partial_term)
        block_shape = (head_count, local_rows // BLOCK, BLOCK, width)
        diagonal = jax.checkpoint(partial(block_term, 1.0))(
            query32.reshape(block_shape), key32.reshape(block_shape), value32.reshape(block_shape)
        )
        summary = combine(summary, diagonal)
        return to_heads(summary[2] / summary[1][..., None])

    query32 = query_rows.astype(jnp.float32)
    key32 = key_rows.astype(jnp.float32)
    value32 = value_rows.astype(jnp.float32)
    pieces, piece_pullback = jax.vjp(own_pieces, key32, value32)
    outbound = {height: pieces[height].astype(jnp.bfloat16) for height in remote}
    received = {
        height: fetch_sibling(outbound[height], partner_bits[height], position) for height in remote
    }
    received32 = {height: received[height].astype(jnp.float32) for height in remote}
    attention, pullback = jax.vjp(local_attention, query32, key32, value32, received32)
    query_grad, key_grad, value_grad, block_grads = pullback(out_grad.astype(jnp.float32))
    piece_grads = {
        height: return_sibling(block_grads[height], partner_bits[height], position)
        for height in remote
    }
    key_extra, value_extra = piece_pullback(piece_grads)
    return (
        attention.astype(jnp.bfloat16),
        query_grad.astype(jnp.bfloat16),
        (key_grad + key_extra).astype(jnp.bfloat16),
        (value_grad + value_extra).astype(jnp.bfloat16),
    )


def solution(mesh):
    placed = (
        P(("groups", "seq"), None, None),
        P(("groups", "seq"), None, None),
        P(("groups", "seq"), None, None),
        P(("groups", "seq"), None, None),
    )
    return jax.shard_map(
        on_device,
        mesh=mesh,
        in_specs=placed,
        out_specs=(
            P(("groups", "seq"), None, None),
            P(("groups", "seq"), None, None),
            P(("groups", "seq"), None, None),
            P(("groups", "seq"), None, None),
        ),
        check_vma=False,
    )
```

profile of v0, /device:TPU:0, one launch (start us, length us, event | category | flops | bytes accessed | tf_op | source)
XLA Modules:
  0.0 216.4 jit_solution(14367803733487058660)
XLA Ops:
  2.0 4.1 %collective-permute-start = (bf16[16,2,8,128]{3,0,2,1:T(8,128)(2,1)S(1)}, bf16[16,2,8,128]{3,0,2,1:T(8,128)(2,1)S(1)}, u32[]{:S(2)}, u32[]{:S(2)}) collective-permute-start(bf16[16,2,8,128]{3,0,2,1:T(8,128)(2,1)S(1)} %pad_maximum_fusion.3), channel_id=1, source_target_pairs={{0,8},{1,9},{2,10},{3,11},{4,12},{5,13},{6,14},{7,15},{8,0},{9,1},... | collective-permute-start | bytes 196616 | tf_op jit(solution)/shard_map/ppermute | solution.py:12
  6.5 1.6 collective-permute-start.4
  9.3 1.5 collective-permute-start.7
  17.3 1.4 fusion.15
  18.7 1.5 fusion.16
  23.7 4.9 %collective-permute-done.2 = bf16[32,2,8,128]{3,0,2,1:T(8,128)(2,1)S(1)} collective-permute-done((bf16[32,2,8,128]{3,0,2,1:T(8,128)(2,1)S(1)}, bf16[32,2,8,128]{3,0,2,1:T(8,128)(2,1)S(1)}, u32[]{:S(2)}, u32[]{:S(2)}) %collective-permute-start.2) | collective-permute-done | bytes 131104 | tf_op jit(solution)/shard_map/ppermute | solution.py:12
  31.9 4.8 %collective-permute-done.3 = bf16[64,2,8,128]{3,0,2,1:T(8,128)(2,1)} collective-permute-done((bf16[64,2,8,128]{3,0,2,1:T(8,128)(2,1)S(1)}, bf16[64,2,8,128]{3,0,2,1:T(8,128)(2,1)}, u32[]{:S(2)}, u32[]{:S(2)}) %collective-permute-start.3) | collective-permute-done | bytes 262176 | tf_op jit(solution)/shard_map/ppermute | solution.py:12
  45.9 1.4 copy.751
  49.9 1.4 copy.785
  52.6 1.4 copy.786
  53.9 1.4 copy.752
  57.6 1.4 maximum_select_fusion.2
  66.2 1.9 fusion.179
  68.1 1.4 copy.819
  69.6 1.5 fusion.81
  72.9 1.4 copy.808
  79.9 1.5 fusion.6
  82.5 1.4 copy.790
  83.9 1.4 copy.762
  85.3 1.5 broadcast_in_dim.159
  86.8 1.6 copy.791
  88.4 1.5 broadcast_in_dim.151
  89.9 1.6 copy.765
  92.2 1.4 multiply_divide_fusion
  93.6 1.5 copy.793
  96.7 1.5 copy.770
  98.9 1.5 copy.780
  100.4 3.2 %bitcast_reduce_fusion = f32[8,128,128]{2,0,1:T(8,128)} fusion(f32[8,256]{0,1:T(8,128)} %copy.770, f32[8,256]{0,1:T(8,128)} %copy.768, f32[8,256]{0,1:T(8,128)} %copy.792, bf16[256,8,128]{2,1,0:T(8,128)(2,1)} %param.7), kind=kLoop, calls=%fused_computation.82 | loop fusion | flops 1179648 | bytes 1073152 | tf_op jit(solution)/shard_map/transpose(jvp())/reduce_sum | solution.py:82
  103.6 4.8 %fusion.71 = (bf16[256,8,128]{2,1,0:T(8,128)(2,1)}, f32[8,256,128]{2,0,1:T(8,128)S(1)}) fusion(f32[8,256]{0,1:T(8,128)S(1)} %copy-done.43, f32[8,256,128]{2,1,0:T(8,128)} %bitcast.431, f32[8,256]{0,1:T(8,128)} %copy.780, f32[8,256,128]{2,1,0:T(8,128)S(1)} %bitcast.430, f32[8,256]{0,1:T(8,128)S(1)} %copy-done.56, f32[8,128,128]{2,0,1:T(8,128)} %copy.775, ...), kind=kLoop, calls=%fused_computation.176 | loop fusion | flops 2097152 | bytes 4235264 | tf_op jit(solution)/shard_map/convert_element_type | solution.py:182
  109.8 1.6 copy.794
  112.7 1.5 copy.812
  114.1 2.0 fusion.117
  117.0 2.2 %multiply_reduce_fusion.3 = (f32[8,64]{0,1:T(8,128)}, f32[8,64,2]{0,2,1:T(2,128)}) fusion(f32[8,64,2]{0,2,1:T(2,128)} %bitcast.439, f32[8,64,2]{0,2,1:T(2,128)} %bitcast.450, f32[8,64]{0,1:T(8,128)} %copy-done.75), kind=kLoop, calls=%fused_computation.286 | loop fusion | flops 3584 | bytes 16384 | tf_op jit(solution)/shard_map/transpose(jvp())/reduce_sum | solution.py:82
  136.9 2.4 %multiply_multiply_fusion.1 = (bf16[8,256,128]{2,0,1:T(8,128)(2,1)}, bf16[8,256,128]{2,0,1:T(8,128)(2,1)}) fusion(f32[8,256]{0,1:T(8,128)S(1)} %copy-done.57, f32[8,256]{0,1:T(8,128)S(1)} %copy-done.46, f32[8,256]{0,1:T(8,128)S(1)} %copy-done.44, bf16[256,8,128]{2,1,0:T(8,128)(2,1)S(1)} %copy-done.16, f32[8,256]{0,1:T(8,128)S(1)} %copy-done.58), kind=kLoop, calls=%fused_computation.131 | loop fusion | flops 1835008 | bytes 1605632 | tf_op jit(solution)/shard_map/transpose(jvp())/mul | solution.py:77
  161.9 1.4 convolution_add_fusion.2
  163.3 2.4 %reverse.6 = f32[8,2,128,128]{3,2,1,0:T(8,128)} reverse(f32[8,2,128,128]{3,2,1,0:T(8,128)} %fusion.33), dimensions={1} | reverse | bytes 2097152 | tf_op jit(solution)/shard_map/reverse
  165.7 2.4 %fusion.17 = f32[8,2,128,128]{3,2,1,0:T(8,128)} fusion(bf16[8,2,128,128]{2,3,1,0:T(8,128)(2,1)} %fusion.50, bf16[8,2,128,128]{3,0,2,1:T(8,128)(2,1)S(1)} %bitcast.429, f32[8,2,128,128]{2,3,1,0:T(8,128)S(1)} %get-tuple-element.90, f32[8,2,128]{2,1,0:T(2,128)S(1)} %get-tuple-element.89), kind=kOutput, calls=%fused_computation.66 | convolution fusion | flops 68157440 | bytes 3153920 | tf_op jit(solution)/shard_map/transpose(jvp(jvp()))/checkpoint/hbqk,hbkd->hbqd/dot_general | solution.py:54
  168.1 2.3 %reverse.7 = f32[8,2,128,128]{3,2,1,0:T(8,128)} reverse(f32[8,2,128,128]{3,2,1,0:T(8,128)} %fusion.17), dimensions={1} | reverse | bytes 2097152 | tf_op jit(solution)/shard_map/reverse.1
  170.4 1.4 pad_add_fusion
  172.2 1.4 fusion.22
  173.7 1.5 convolution_add_fusion
  177.5 1.6 collective-permute-start.18
  182.5 14.8 %collective-permute-done.11 = f32[32,2,8,128]{3,0,2,1:T(8,128)S(1)} collective-permute-done((f32[32,2,8,128]{3,0,2,1:T(8,128)S(1)}, f32[32,2,8,128]{3,0,2,1:T(8,128)S(1)}, u32[]{:S(2)}, u32[]{:S(2)}) %collective-permute-start.11) | collective-permute-done | bytes 262176 | tf_op jit(solution)/shard_map/ppermute | solution.py:12
  198.2 1.6 collective-permute-start.16
  201.7 7.3 %collective-permute-done.13 = f32[16,2,8,128]{3,0,2,1:T(8,128)S(1)} collective-permute-done((f32[16,2,8,128]{3,0,2,1:T(8,128)S(1)}, f32[16,2,8,128]{3,0,2,1:T(8,128)S(1)}, u32[]{:S(2)}, u32[]{:S(2)}) %collective-permute-start.13) | collective-permute-done | bytes 131104 | tf_op jit(solution)/shard_map/ppermute | solution.py:12
  210.2 1.4 copy.843
  213.5 1.4 fusion.19
  215.0 1.4 fusion.21
  (433 shorter events, 105.3 us)
Async XLA Ops:
  1.9 4.3 %copy-start.1 = (bf16[256,8,128]{2,1,0:T(8,128)(2,1)S(1)}, bf16[256,8,128]{2,1,0:T(8,128)(2,1)}, u32[]{:S(2)}) copy-start(bf16[256,8,128]{2,1,0:T(8,128)(2,1)} %param.5) | copy-start | bytes 1572868
  2.0 18.3 %collective-permute-start = (bf16[16,2,8,128]{3,0,2,1:T(8,128)(2,1)S(1)}, bf16[16,2,8,128]{3,0,2,1:T(8,128)(2,1)S(1)}, u32[]{:S(2)}, u32[]{:S(2)}) collective-permute-start(bf16[16,2,8,128]{3,0,2,1:T(8,128)(2,1)S(1)} %pad_maximum_fusion.3), channel_id=1, source_target_pairs={{0,8},{1,9},{2,10},{3,11},{4,12},{5,13},{6,14},{7,15},{8,0},{9,1},... | collective-permute-start | bytes 196616 | tf_op jit(solution)/shard_map/ppermute | solution.py:12
  6.5 17.1 %collective-permute-start.4 = (bf16[32,2,8,128]{3,0,2,1:T(8,128)(2,1)S(1)}, bf16[32,2,8,128]{3,0,2,1:T(8,128)(2,1)}, u32[]{:S(2)}, u32[]{:S(2)}) collective-permute-start(bf16[32,2,8,128]{3,0,2,1:T(8,128)(2,1)S(1)} %pad_maximum_fusion.2), channel_id=1, source_target_pairs={{0,4},{1,5},{2,6},{3,7},{4,0},{5,1},{6,2},{7,3},{8,12},{9,13},{10,... | collective-permute-start | bytes 393224 | tf_op jit(solution)/shard_map/ppermute | solution.py:12
  9.3 22.6 %collective-permute-start.7 = (bf16[64,2,8,128]{3,0,2,1:T(8,128)(2,1)}, bf16[64,2,8,128]{3,0,2,1:T(8,128)(2,1)}, u32[]{:S(2)}, u32[]{:S(2)}) collective-permute-start(bf16[64,2,8,128]{3,0,2,1:T(8,128)(2,1)} %pad_maximum_fusion.1), channel_id=1, source_target_pairs={{0,2},{1,3},{2,0},{3,1},{4,6},{5,7},{6,4},{7,5},{8,10},{9,11},{10,... | collective-permute-start | bytes 786440 | tf_op jit(solution)/shard_map/ppermute | solution.py:12
  12.4 53.8 %collective-permute-start.9 = (bf16[128,2,8,128]{3,0,2,1:T(8,128)(2,1)}, bf16[128,2,8,128]{3,0,2,1:T(8,128)(2,1)}, u32[]{:S(2)}, u32[]{:S(2)}) collective-permute-start(bf16[128,2,8,128]{3,0,2,1:T(8,128)(2,1)} %pad_maximum_fusion), channel_id=1, source_target_pairs={{0,1},{1,0},{2,3},{3,2},{4,5},{5,4},{6,7},{7,6},{8,9},{9,8},{10,11... | collective-permute-start | bytes 1572872 | tf_op jit(solution)/shard_map/ppermute | solution.py:12
  14.7 2.6 %copy-start.17 = (bf16[8,2,128,128]{3,2,1,0:T(8,128)(2,1)}, bf16[8,2,128,128]{3,2,1,0:T(8,128)(2,1)S(1)}, u32[]{:S(2)}) copy-start(bf16[8,2,128,128]{3,2,1,0:T(8,128)(2,1)S(1)} %get-tuple-element.20) | copy-start | bytes 1572868
  20.3 17.5 %copy-start.65 = (f32[8,16,128]{2,0,1:T(8,128)}, f32[8,16,128]{2,0,1:T(8,128)S(1)}, u32[]{:S(2)}) copy-start(f32[8,16,128]{2,0,1:T(8,128)S(1)} %bitcast_reduce_fusion.12) | copy-start | bytes 196612
  20.3 2.4 %collective-permute-start.1 = (bf16[16,2,8,128]{3,0,2,1:T(8,128)(2,1)S(1)}, bf16[16,2,8,128]{3,0,2,1:T(8,128)(2,1)S(1)}, u32[]{:S(2)}, u32[]{:S(2)}) collective-permute-start(bf16[16,2,8,128]{3,0,2,1:T(8,128)(2,1)S(1)} %collective-permute-done), channel_id=1, source_target_pairs={{0,1},{1,0},{2,3},{3,2},{4,5},{5,4},{6,7},{7,6},{8,9},{9,8},{10,11... | collective-permute-start | bytes 196616 | tf_op jit(solution)/shard_map/ppermute | solution.py:12
  22.8 5.8 %collective-permute-start.2 = (bf16[32,2,8,128]{3,0,2,1:T(8,128)(2,1)S(1)}, bf16[32,2,8,128]{3,0,2,1:T(8,128)(2,1)S(1)}, u32[]{:S(2)}, u32[]{:S(2)}) collective-permute-start(bf16[32,2,8,128]{3,0,2,1:T(8,128)(2,1)S(1)} %maximum_select_fusion.5), channel_id=1, source_target_pairs={{0,2},{1,3},{2,0},{3,1},{4,6},{5,7},{6,4},{7,5},{8,10},{9,11},{10,... | collective-permute-start | bytes 393224 | tf_op jit(solution)/shard_map/ppermute | solution.py:12
  23.5 6.6 %collective-permute-start.5 = (bf16[32,2,8,128]{3,0,2,1:T(8,128)(2,1)}, bf16[32,2,8,128]{3,0,2,1:T(8,128)(2,1)}, u32[]{:S(2)}, u32[]{:S(2)}) collective-permute-start(bf16[32,2,8,128]{3,0,2,1:T(8,128)(2,1)} %collective-permute-done.4), channel_id=1, source_target_pairs={{0,1},{1,0},{2,3},{3,2},{4,5},{5,4},{6,7},{7,6},{8,9},{9,8},{10,11... | collective-permute-start | bytes 393224 | tf_op jit(solution)/shard_map/ppermute | solution.py:12
  28.7 7.9 %collective-permute-start.3 = (bf16[64,2,8,128]{3,0,2,1:T(8,128)(2,1)S(1)}, bf16[64,2,8,128]{3,0,2,1:T(8,128)(2,1)}, u32[]{:S(2)}, u32[]{:S(2)}) collective-permute-start(bf16[64,2,8,128]{3,0,2,1:T(8,128)(2,1)S(1)} %maximum_select_fusion.3), channel_id=1, source_target_pairs={{0,4},{1,5},{2,6},{3,7},{4,0},{5,1},{6,2},{7,3},{8,12},{9,13},{10,... | collective-permute-start | bytes 786440 | tf_op jit(solution)/shard_map/ppermute | solution.py:12
  31.3 6.6 %copy-start.73 = (bf16[8,16,128]{2,1,0:T(8,128)(2,1)S(1)}, bf16[8,16,128]{2,1,0:T(8,128)(2,1)}, u32[]{:S(2)}) copy-start(bf16[8,16,128]{2,1,0:T(8,128)(2,1)} %fusion.139) | copy-start | bytes 98308
  31.3 8.2 %collective-permute-start.6 = (bf16[64,2,8,128]{3,0,2,1:T(8,128)(2,1)S(1)}, bf16[64,2,8,128]{3,0,2,1:T(8,128)(2,1)S(1)}, u32[]{:S(2)}, u32[]{:S(2)}) collective-permute-start(bf16[64,2,8,128]{3,0,2,1:T(8,128)(2,1)S(1)} %maximum_select_fusion.4), channel_id=1, source_target_pairs={{0,2},{1,3},{2,0},{3,1},{4,6},{5,7},{6,4},{7,5},{8,10},{9,11},{10,... | collective-permute-start | bytes 786440 | tf_op jit(solution)/shard_map/ppermute | solution.py:12
  31.9 25.7 %collective-permute-start.8 = (bf16[64,2,8,128]{3,0,2,1:T(8,128)(2,1)}, bf16[64,2,8,128]{3,0,2,1:T(8,128)(2,1)}, u32[]{:S(2)}, u32[]{:S(2)}) collective-permute-start(bf16[64,2,8,128]{3,0,2,1:T(8,128)(2,1)} %collective-permute-done.7), channel_id=1, source_target_pairs={{0,1},{1,0},{2,3},{3,2},{4,5},{5,4},{6,7},{7,6},{8,9},{9,8},{10,11... | collective-permute-start | bytes 786440 | tf_op jit(solution)/shard_map/ppermute | solution.py:12
  40.3 16.3 %copy-start.32 = (bf16[128,2,8,128]{3,0,2,1:T(8,128)(2,1)}, bf16[128,2,8,128]{3,0,2,1:T(8,128)(2,1)S(1)}, u32[]{:S(2)}) copy-start(bf16[128,2,8,128]{3,0,2,1:T(8,128)(2,1)S(1)} %maximum_select_fusion.1) | copy-start | bytes 1572868
  40.7 2.0 copy-start.88
  59.3 3.5 %copy-start.27 = (f32[8,64,128]{2,1,0:T(8,128)}, f32[8,64,128]{2,1,0:T(8,128)S(1)}, u32[]{:S(2)}) copy-start(f32[8,64,128]{2,1,0:T(8,128)S(1)} %get-tuple-element.82) | copy-start | bytes 786436
  60.8 4.9 %copy-start.106 = (f32[8,64]{1,0:T(8,128)}, f32[8,64]{1,0:T(8,128)S(1)}, u32[]{:S(2)}) copy-start(f32[8,64]{1,0:T(8,128)S(1)} %get-tuple-element.44) | copy-start | bytes 6148
  100.4 3.2 %copy-start.24 = (f32[8,2,128,128]{3,2,1,0:T(8,128)S(1)}, f32[8,2,128,128]{3,2,1,0:T(8,128)}, u32[]{:S(2)}) copy-start(f32[8,2,128,128]{3,2,1,0:T(8,128)} %fusion.15) | copy-start | bytes 3145732
  100.4 3.2 %copy-start.43 = (f32[8,256]{0,1:T(8,128)S(1)}, f32[8,256]{0,1:T(8,128)}, u32[]{:S(2)}) copy-start(f32[8,256]{0,1:T(8,128)} %copy.792) | copy-start | bytes 24580
  100.4 3.2 %copy-start.45 = (f32[8,256]{0,1:T(8,128)S(1)}, f32[8,256]{0,1:T(8,128)}, u32[]{:S(2)}) copy-start(f32[8,256]{0,1:T(8,128)} %copy.768) | copy-start | bytes 24580
  100.4 3.2 %copy-start.56 = (f32[8,256]{0,1:T(8,128)S(1)}, f32[8,256]{0,1:T(8,128)}, u32[]{:S(2)}) copy-start(f32[8,256]{0,1:T(8,128)} %copy.776) | copy-start | bytes 24580
  103.6 4.9 %copy-start.15 = (bf16[256,8,128]{2,1,0:T(8,128)(2,1)S(1)}, bf16[256,8,128]{2,1,0:T(8,128)(2,1)}, u32[]{:S(2)}) copy-start(bf16[256,8,128]{2,1,0:T(8,128)(2,1)} %param.7) | copy-start | bytes 1572868
  103.6 4.9 %copy-start.72 = (f32[8,256]{0,1:T(8,128)S(1)}, f32[8,256]{0,1:T(8,128)}, u32[]{:S(2)}) copy-start(f32[8,256]{0,1:T(8,128)} %copy.793) | copy-start | bytes 24580
  120.0 2.0 copy-start.97
  133.0 1.9 copy-start.20
  134.9 2.0 copy-start.58
  136.9 2.4 %copy-start.105 = (f32[8,128]{1,0:T(8,128)S(1)}, f32[8,128]{1,0:T(8,128)}, u32[]{:S(2)}) copy-start(f32[8,128]{1,0:T(8,128)} %copy-done.104) | copy-start | bytes 12292
  136.9 2.4 %copy-start.23 = (f32[8,128,128]{2,0,1:T(8,128)S(1)}, f32[8,128,128]{2,0,1:T(8,128)}, u32[]{:S(2)}) copy-start(f32[8,128,128]{2,0,1:T(8,128)} %bitcast_reduce_fusion) | copy-start | bytes 1572868
  136.9 2.4 %copy-start.79 = (f32[8,128]{0,1:T(8,128)S(1)}, f32[8,128]{0,1:T(8,128)}, u32[]{:S(2)}) copy-start(f32[8,128]{0,1:T(8,128)} %copy.808) | copy-start | bytes 12292
  148.7 2.5 %copy-start.3 = (f32[128,1,8,128]{3,0,2,1:T(8,128)S(1)}, f32[128,1,8,128]{3,0,2,1:T(8,128)}, u32[]{:S(2)}) copy-start(f32[128,1,8,128]{3,0,2,1:T(8,128)} %convolution_bitcast_fusion.1) | copy-start | bytes 1572868
  148.7 2.5 %copy-start.7 = (f32[128,1,8,128]{3,0,2,1:T(8,128)S(1)}, f32[128,1,8,128]{3,0,2,1:T(8,128)}, u32[]{:S(2)}) copy-start(f32[128,1,8,128]{3,0,2,1:T(8,128)} %convolution_bitcast_fusion) | copy-start | bytes 1572868
  152.1 1.9 copy-start.11
  152.1 1.9 copy-start.13
  152.1 23.3 %collective-permute-start.17 = (f32[64,2,8,128]{3,0,2,1:T(8,128)}, f32[64,2,8,128]{3,0,2,1:T(8,128)}, u32[]{:S(2)}, u32[]{:S(2)}) collective-permute-start(f32[64,2,8,128]{3,0,2,1:T(8,128)} %fusion.60), channel_id=1, source_target_pairs={{0,1},{1,0},{2,3},{3,2},{4,5},{5,4},{6,7},{7,6},{8,9},{9,8},{10,11... | collective-permute-start | bytes 1572872 | tf_op jit(solution)/shard_map/ppermute | solution.py:12
  153.5 27.4 %collective-permute-start.14 = (f32[64,2,8,128]{3,0,2,1:T(8,128)}, f32[64,2,8,128]{3,0,2,1:T(8,128)}, u32[]{:S(2)}, u32[]{:S(2)}) collective-permute-start(f32[64,2,8,128]{3,0,2,1:T(8,128)} %fusion.57), channel_id=1, source_target_pairs={{0,2},{1,3},{2,0},{3,1},{4,6},{5,7},{6,4},{7,5},{8,10},{9,11},{10,... | collective-permute-start | bytes 1572872 | tf_op jit(solution)/shard_map/ppermute | solution.py:12
  154.9 24.1 %collective-permute-start.10 = (f32[64,2,8,128]{3,0,2,1:T(8,128)}, f32[64,2,8,128]{3,0,2,1:T(8,128)}, u32[]{:S(2)}, u32[]{:S(2)}) collective-permute-start(f32[64,2,8,128]{3,0,2,1:T(8,128)} %fusion.54), channel_id=1, source_target_pairs={{0,4},{1,5},{2,6},{3,7},{4,0},{5,1},{6,2},{7,3},{8,12},{9,13},{10,... | collective-permute-start | bytes 1572872 | tf_op jit(solution)/shard_map/ppermute | solution.py:12
  163.3 2.4 %copy-start.22 = (bf16[8,256,128]{2,0,1:T(8,128)(2,1)S(1)}, bf16[8,256,128]{2,0,1:T(8,128)(2,1)}, u32[]{:S(2)}) copy-start(bf16[8,256,128]{2,0,1:T(8,128)(2,1)} %get-tuple-element.19) | copy-start | bytes 1572868
  171.8 37.2 %collective-permute-start.19 = (f32[128,2,8,128]{0,3,2,1:T(8,128)S(1)}, f32[128,2,8,128]{0,3,2,1:T(8,128)S(1)}, u32[]{:S(2)}, u32[]{:S(2)}) collective-permute-start(f32[128,2,8,128]{0,3,2,1:T(8,128)S(1)} %pad_add_fusion), channel_id=1, source_target_pairs={{0,1},{1,0},{2,3},{3,2},{4,5},{5,4},{6,7},{7,6},{8,9},{9,8},{10,11... | collective-permute-start | bytes 3145736 | tf_op jit(solution)/shard_map/ppermute | solution.py:12
  175.5 3.6 %copy-start.12 = (f32[128,1,8,128]{3,0,2,1:T(8,128)S(1)}, f32[128,1,8,128]{3,0,2,1:T(8,128)}, u32[]{:S(2)}) copy-start(f32[128,1,8,128]{3,0,2,1:T(8,128)} %convolution_bitcast_fusion.5) | copy-start | bytes 1572868
  175.5 3.5 %copy-start.14 = (f32[128,1,8,128]{3,0,2,1:T(8,128)S(1)}, f32[128,1,8,128]{3,0,2,1:T(8,128)}, u32[]{:S(2)}) copy-start(f32[128,1,8,128]{3,0,2,1:T(8,128)} %convolution_bitcast_fusion.4) | copy-start | bytes 1572868
  177.5 23.2 %collective-permute-start.18 = (f32[64,2,8,128]{3,0,2,1:T(8,128)S(1)}, f32[64,2,8,128]{3,0,2,1:T(8,128)S(1)}, u32[]{:S(2)}, u32[]{:S(2)}) collective-permute-start(f32[64,2,8,128]{3,0,2,1:T(8,128)S(1)} %fusion.62), channel_id=1, source_target_pairs={{0,2},{1,3},{2,0},{3,1},{4,6},{5,7},{6,4},{7,5},{8,10},{9,11},{10,... | collective-permute-start | bytes 1572872 | tf_op jit(solution)/shard_map/ppermute | solution.py:12
  180.3 17.0 %collective-permute-start.11 = (f32[32,2,8,128]{3,0,2,1:T(8,128)S(1)}, f32[32,2,8,128]{3,0,2,1:T(8,128)S(1)}, u32[]{:S(2)}, u32[]{:S(2)}) collective-permute-start(f32[32,2,8,128]{3,0,2,1:T(8,128)S(1)} %constant_dynamic-slice_fusion.2), channel_id=1, source_target_pairs={{0,2},{1,3},{2,0},{3,1},{4,6},{5,7},{6,4},{7,5},{8,10},{9,11},{10,... | collective-permute-start | bytes 786440 | tf_op jit(solution)/shard_map/ppermute | solution.py:12
  182.4 15.0 %collective-permute-start.15 = (f32[32,2,8,128]{3,0,2,1:T(8,128)S(1)}, f32[32,2,8,128]{3,0,2,1:T(8,128)S(1)}, u32[]{:S(2)}, u32[]{:S(2)}) collective-permute-start(f32[32,2,8,128]{3,0,2,1:T(8,128)S(1)} %constant_dynamic-slice_fusion), channel_id=1, source_target_pairs={{0,1},{1,0},{2,3},{3,2},{4,5},{5,4},{6,7},{7,6},{8,9},{9,8},{10,11... | collective-permute-start | bytes 786440 | tf_op jit(solution)/shard_map/ppermute | solution.py:12
  197.3 2.4 %collective-permute-start.12 = (f32[16,2,8,128]{3,0,2,1:T(8,128)S(1)}, f32[16,2,8,128]{3,0,2,1:T(8,128)S(1)}, u32[]{:S(2)}, u32[]{:S(2)}) collective-permute-start(f32[16,2,8,128]{3,0,2,1:T(8,128)S(1)} %constant_dynamic-slice_fusion.1), channel_id=1, source_target_pairs={{0,1},{1,0},{2,3},{3,2},{4,5},{5,4},{6,7},{7,6},{8,9},{9,8},{10,11... | collective-permute-start | bytes 393224 | tf_op jit(solution)/shard_map/ppermute | solution.py:12
  198.2 13.4 %collective-permute-start.16 = (f32[32,2,8,128]{3,0,2,1:T(8,128)}, f32[32,2,8,128]{3,0,2,1:T(8,128)}, u32[]{:S(2)}, u32[]{:S(2)}) collective-permute-start(f32[32,2,8,128]{3,0,2,1:T(8,128)} %dynamic-slice_add_fusion), channel_id=1, source_target_pairs={{0,4},{1,5},{2,6},{3,7},{4,0},{5,1},{6,2},{7,3},{8,12},{9,13},{10,... | collective-permute-start | bytes 786440 | tf_op jit(solution)/shard_map/ppermute | solution.py:12
  199.8 9.2 %collective-permute-start.13 = (f32[16,2,8,128]{3,0,2,1:T(8,128)S(1)}, f32[16,2,8,128]{3,0,2,1:T(8,128)S(1)}, u32[]{:S(2)}, u32[]{:S(2)}) collective-permute-start(f32[16,2,8,128]{3,0,2,1:T(8,128)S(1)} %dynamic-slice_add_fusion.2), channel_id=1, source_target_pairs={{0,8},{1,9},{2,10},{3,11},{4,12},{5,13},{6,14},{7,15},{8,0},{9,1},... | collective-permute-start | bytes 393224 | tf_op jit(solution)/shard_map/ppermute | solution.py:12
  210.2 2.6 %copy-start.30 = (f32[8,2,128,128]{3,2,1,0:T(8,128)S(1)}, f32[8,2,128,128]{3,2,1,0:T(8,128)}, u32[]{:S(2)}) copy-start(f32[8,2,128,128]{3,2,1,0:T(8,128)} %convolution_add_fusion) | copy-start | bytes 3145732
  (93 other events, 106.8 us)
where the time goes:
time: 219 us; the launch traced here: 216 us
  local copies, waits for them, and re-layouts  71 us (32%)
  other arithmetic  61.8 us (28%)
  matrix products  34.8 us (16%)
  waiting for transfers between devices  31.8 us (15%)
  starting transfers between devices  15.1 us (7%)
    ppermute x20, waiting for transfers between devices, partner_2(): lax.ppermute(array, axis, [(i, i ^ 1 << stride) for i in range(lax.axis_s...  31.8 us
    dot_general x18, matrix products, block_term(): jnp.einsum('hbqk,hbkd->hbqd', keep_round(weights), value_blocks, precisio...  19 us
    dot_general x20, matrix products, block_term(): jnp.einsum('hbqd,hbkd->hbqk', query_blocks, key_blocks, precision=lax.Pre...  15.8 us
    ppermute x20, starting transfers between devices, partner_2(): lax.ppermute(array, axis, [(i, i ^ 1 << stride) for i in range(lax.axis_s...  15.1 us
    unnamed x242, local copies, waits for them, and re-layouts  14.6 us
    convert_element_type x20, other arithmetic, keep_round(): lowered = lax.optimization_barrier(frozen.astype(jnp.bfloat16))  11.2 us
    reduce_sum x8, other arithmetic, upsample(): return tuple((jnp.repeat(entry, 2, axis=1) for entry in summary))  10.6 us
    reshape x8, local copies, waits for them, and re-layouts, upsample(): return tuple((jnp.repeat(entry, 2, axis=1) for entry in summary))  8.08 us
  transfers between devices with their start and end apart: 20, of which 4 were waited for; matrix products, arithmetic and copies ran while one was open for 33% of the time, Pallas kernels for 0%

commit v1 on v0

v1 whole, which is shorter than its diff:
```python
from functools import partial

import jax
import jax.numpy as jnp
from jax import lax
from jax.experimental import pallas as pl
from jax.experimental.pallas import tpu as pltpu
from jax.sharding import PartitionSpec as P

BLOCK = 128
CHUNK = 16
F32 = jnp.float32
BF16 = jnp.bfloat16
MESH = pl.DeviceIdType.MESH


def bit_reversed(value, bits):
    return sum(((value >> bit) & 1) << (bits - 1 - bit) for bit in range(bits))


def load_rows(ref, head, heads, level):
    bits = max(4 - level, 0)
    parts = [
        ref[pl.ds(bit_reversed(b, bits) * heads + head, CHUNK, stride=heads << bits), :]
        for b in range(1 << bits)
    ]
    return parts[0] if len(parts) == 1 else jnp.concatenate(parts, 0)


def store_rows(ref, head, heads, level, values):
    bits = max(4 - level, 0)
    for b in range(1 << bits):
        ref[pl.ds(bit_reversed(b, bits) * heads + head, CHUNK, stride=heads << bits), :] = values[
            b * CHUNK : (b + 1) * CHUNK
        ]


def dot_nt(a, b):
    return lax.dot_general(a, b, (((1,), (1,)), ((), ())), preferred_element_type=F32)


def dot_nn(a, b):
    return lax.dot_general(a, b, (((1,), (0,)), ((), ())), preferred_element_type=F32)


def dot_tn(a, b):
    return lax.dot_general(a, b, (((0,), (0,)), ((), ())), preferred_element_type=F32)


def pair_sum(x):
    return jnp.sum(x.reshape((x.shape[0] // 2, 2) + x.shape[1:]), axis=1)


def repeat_rows(x, times):
    spread = jnp.broadcast_to(x[:, None], (x.shape[0], times) + x.shape[1:])
    return spread.reshape((x.shape[0] * times,) + x.shape[1:])


def kernel(levels, heads, width, rows, *refs):
    q_ref, k_ref, v_ref, g_ref, o_ref, dq_ref, dk_ref, dv_ref = refs[:8]
    (q32, k32, v32, g32, att32, tops, high, p0, num0, m0, l0, c0, d0) = refs[8:21]
    (sem_out, sem_in, sem_fwd_out, sem_fwd_in) = refs[21:25]
    (sem_half_out, sem_half_in, sem_back_out, sem_back_in) = refs[25:29]
    per = levels - 1
    cut = 29
    groups = [dict(zip(range(1, levels), refs[cut + i * per : cut + (i + 1) * per])) for i in range(7)]
    ql, own, got, kv32, give, gain, total = groups
    back = dict(zip(range(1, levels), refs[cut + 7 * per : cut + 8 * per]))
    factor = width ** (-0.5)
    remote = list(range(1, levels))
    wide = [level for level in remote if level >= 2]
    chunks = rows // CHUNK
    half = BLOCK // 2

    me = lax.axis_index("seq")
    core = me % 2
    sibling = me + 1 - 2 * core

    def partners(level):
        span = 1 << (level - 1)
        block = me // span
        base = (block + 1 - 2 * (block % 2)) * span
        return [base + 2 * j + core for j in range(span // 2)]

    def place(level):
        return (me % (1 << (level - 1))) // 2

    barrier = pltpu.get_barrier_semaphore()
    peers = [sibling] + [peer for level in wide for peer in partners(level)]
    for peer in peers:
        pl.semaphore_signal(barrier, inc=1, device_id={"seq": peer}, device_id_type=MESH)

    def remote_copy(src, dst, send, recv, peer):
        return pltpu.make_async_remote_copy(
            src_ref=src, dst_ref=dst, send_sem=send, recv_sem=recv,
            device_id={"seq": peer}, device_id_type=MESH,
        )

    def prepare_kv(i, carry):
        for which, (ref, store) in enumerate(((k_ref, k32), (v_ref, v32))):
            x = ref[pl.ds(i * CHUNK, CHUNK)].astype(F32)
            store[pl.ds(i * CHUNK * heads, CHUNK * heads), :] = x.reshape(CHUNK * heads, width)
            for level in range(1, min(levels, 5)):
                x = pair_sum(x)
                n = CHUNK >> level
                own[level][which, pl.ds(i * n, n)] = (x * 0.5**level).astype(BF16)
            if levels > 5:
                tops[which, pl.ds(i, 1)] = x
        return carry

    lax.fori_loop(0, chunks, prepare_kv, 0)
    for which in range(2):
        if levels > 5:
            x = tops[which]
            for level in range(5, levels):
                x = pair_sum(x)
                own[level][which] = (x * 0.5**level).astype(BF16)

    pl.semaphore_wait(barrier, len(peers))
    sends = []
    slot = 0
    for level in sorted(wide, reverse=True):
        n = rows >> level
        at = place(level) * n
        for peer in partners(level):
            sends.append(
                remote_copy(
                    own[level], got[level].at[core, :, pl.ds(at, n)],
                    sem_out.at[slot], sem_in.at[level], peer,
                )
            )
            sends[-1].start()
            slot += 1
    first = remote_copy(own[1], got[1].at[0], sem_out.at[slot], sem_in.at[1], sibling)
    first.start()

    def prepare_q(i, carry):
        x = q_ref[pl.ds(i * CHUNK, CHUNK)].astype(F32)
        q32[pl.ds(i * CHUNK * heads, CHUNK * heads), :] = x.reshape(CHUNK * heads, width)
        for level in range(1, min(levels, 5)):
            x = pair_sum(x)
            n = CHUNK >> level
            lowered = (x * 0.5**level).astype(BF16).astype(F32)
            ql[level][pl.ds(i * n * heads, n * heads), :] = lowered.reshape(n * heads, width)
        if levels > 5:
            tops[2, pl.ds(i, 1)] = x
        g = g_ref[pl.ds(i * CHUNK, CHUNK)].astype(F32)
        g32[pl.ds(i * CHUNK * heads, CHUNK * heads), :] = g.reshape(CHUNK * heads, width)
        return carry

    lax.fori_loop(0, chunks, prepare_q, 0)
    if levels > 5:
        x = tops[2]
        for level in range(5, levels):
            x = pair_sum(x)
            lowered = repeat_rows((x * 0.5**level).astype(BF16).astype(F32), 1 << (level - 4))
            ql[level][...] = lowered.reshape(CHUNK * heads, width)

    def near_forward(h, carry):
        q = load_rows(q32, h, heads, 0).astype(BF16)
        k = k32[pl.ds(h, rows, stride=heads), :].astype(BF16)
        v = v32[pl.ds(h, rows, stride=heads), :].astype(BF16)
        s = dot_nt(q, k) * factor
        m = jnp.max(s, axis=1, keepdims=True)
        p = jnp.exp(s - m)
        p0[h] = p
        m0[h] = m
        l0[h] = jnp.sum(p, axis=1, keepdims=True)
        num0[h] = dot_nn(p.astype(BF16), v)
        return carry

    lax.fori_loop(0, heads, near_forward, 0)

    forwards = {}
    for level in sorted(wide, reverse=True):
        mine = got[level].at[core]
        remote_copy(mine, mine, sem_out.at[0], sem_in.at[level], sibling).wait_recv()
        forwards[level] = remote_copy(
            mine, mine, sem_fwd_out.at[level], sem_fwd_in.at[level], sibling
        )
        forwards[level].start()
    first.wait_recv()

    def widen(level):
        parts = got[level].shape[0]
        depth = BLOCK // parts

        def body(i, carry):
            n = depth // 8
            for part in range(parts):
                for which in range(2):
                    x = got[level][part, which, pl.ds(i * n, n)].astype(F32)
                    kv32[level][which, pl.ds((part * depth + i * n) * heads, n * heads), :] = x.reshape(
                        n * heads, width
                    )
            return carry

        lax.fori_loop(0, 8, body, 0)

    widen(1)
    for level in sorted(wide, reverse=True):
        other = got[level].at[1 - core]
        remote_copy(other, other, sem_fwd_out.at[level], sem_fwd_in.at[level], sibling).wait_recv()
        widen(level)

    def far(h, carry):
        m_all = den = num = None
        kept = {}
        for level in reversed(remote):
            q = load_rows(ql[level], h, heads, level).astype(BF16)
            k = kv32[level][0, pl.ds(h, BLOCK, stride=heads), :].astype(BF16)
            v = kv32[level][1, pl.ds(h, BLOCK, stride=heads), :].astype(BF16)
            s = dot_nt(q, k) * factor
            m = jnp.max(s, axis=1, keepdims=True)
            p = jnp.exp(s - m)
            pb = p.astype(BF16)
            weight = float(1 << level)
            den_l = jnp.sum(p, axis=1, keepdims=True)
            num_l = dot_nn(pb, v)
            if m_all is None:
                scale_a, scale_b = None, jnp.full(m.shape, weight, F32)
                m_all, den, num = m, den_l * weight, num_l * weight
            else:
                if m_all.shape[0] < m.shape[0]:
                    m_all, den, num = (jnp.concatenate([x, x], 0) for x in (m_all, den, num))
                top = jnp.maximum(m_all, m)
                scale_a = jnp.exp(m_all - top)
                scale_b = jnp.exp(m - top) * weight
                m_all = top
                den = scale_a * den + scale_b * den_l
                num = scale_a * num + scale_b * num_l
            kept[level] = (q, k, v, p, pb, scale_a, scale_b)
        m = m0[h]
        m_all, den, num = (jnp.concatenate([x, x], 0) for x in (m_all, den, num))
        top = jnp.maximum(m_all, m)
        scale_a = jnp.exp(m_all - top)
        scale_b = jnp.exp(m - top)
        den = scale_a * den + scale_b * l0[h]
        num = scale_a * num + scale_b * num0[h]
        inverse = 1.0 / den
        att = num * inverse
        store_rows(att32, h, heads, 0, att)
        g = load_rows(g32, h, heads, 0)
        d = jnp.sum(g * att, axis=1, keepdims=True)
        c0[h] = scale_b * inverse
        d0[h] = d
        scale = scale_a * inverse
        up, up_d = g * scale, d * scale
        for level in remote:
            q, k, v, p, pb, scale_a, scale_b = kept[level]
            if up.shape[0] > q.shape[0]:
                n = q.shape[0]
                up, up_d = up[:n] + up[n:], up_d[:n] + up_d[n:]
            gb = (up * scale_b).astype(BF16)
            ds = (p * (dot_nt(gb, v) - up_d * scale_b) * factor).astype(BF16)
            store_rows(ql[level], h, heads, level, dot_nn(ds, k))
            kv32[level][0, pl.ds(h, BLOCK, stride=heads), :] = dot_tn(ds, q)
            kv32[level][1, pl.ds(h, BLOCK, stride=heads), :] = dot_tn(pb, gb)
            if scale_a is not None:
                up, up_d = up * scale_a, up_d * scale_a
        return carry

    lax.fori_loop(0, heads, far, 0)

    halves = {}
    for level in sorted(wide, reverse=True):

        def narrow(i, carry, level=level):
            n = half // 4
            for which in range(2):
                x = kv32[level][which, pl.ds(((1 - core) * half + i * n) * heads, n * heads), :]
                give[level][which, pl.ds(i * n, n)] = x.reshape(n, heads, width).astype(BF16)
            return carry

        lax.fori_loop(0, 4, narrow, 0)
        halves[level] = remote_copy(
            give[level], gain[level], sem_half_out.at[level], sem_half_in.at[level], sibling
        )
        halves[level].start()

    def narrow_first(i, carry):
        n = BLOCK // 8
        for which in range(2):
            x = kv32[1][which, pl.ds(i * n * heads, n * heads), :]
            give[1][which, pl.ds(i * n, n)] = x.reshape(n, heads, width).astype(BF16)
        return carry

    lax.fori_loop(0, 8, narrow_first, 0)
    first_back = remote_copy(
        give[1], back[1].at[0], sem_half_out.at[1], sem_back_in.at[1], sibling
    )
    first_back.start()

    returns = []
    slot = 0
    for level in sorted(wide, reverse=True):
        halves[level].wait_recv()

        def add(i, carry, level=level):
            n = half // 4
            for which in range(2):
                x = kv32[level][which, pl.ds((core * half + i * n) * heads, n * heads), :]
                y = gain[level][which, pl.ds(i * n, n)].astype(F32)
                total[level][which, pl.ds(i * n, n)] = (x.reshape(n, heads, width) + y).astype(BF16)
            return carry

        lax.fori_loop(0, 4, add, 0)
        n = rows >> level
        for j, peer in enumerate(partners(level)):
            returns.append(
                remote_copy(
                    total[level].at[:, pl.ds(j * n, n)], back[level].at[place(level)],
                    sem_back_out.at[slot], sem_back_in.at[level], peer,
                )
            )
            returns[-1].start()
            slot += 1

    def near_backward(h, carry):
        q = load_rows(q32, h, heads, 0).astype(BF16)
        g = load_rows(g32, h, heads, 0).astype(BF16)
        k = k32[pl.ds(h, rows, stride=heads), :].astype(BF16)
        v = v32[pl.ds(h, rows, stride=heads), :].astype(BF16)
        p = p0[h] * c0[h]
        ds = (p * (dot_nt(g, v) - d0[h]) * factor).astype(BF16)
        store_rows(q32, h, heads, 0, dot_nn(ds, k))
        k32[pl.ds(h, rows, stride=heads), :] = dot_tn(ds, q)
        v32[pl.ds(h, rows, stride=heads), :] = dot_tn(p.astype(BF16), g)
        return carry

    lax.fori_loop(0, heads, near_backward, 0)

    low = range(1, min(levels, 5))

    def finish_q(i, carry):
        o = att32[pl.ds(i * CHUNK * heads, CHUNK * heads), :]
        o_ref[pl.ds(i * CHUNK, CHUNK)] = o.reshape(CHUNK, heads, width).astype(BF16)
        extra = high[0, pl.ds(i, 1)] if levels > 5 else None
        for level in reversed(low):
            n = CHUNK >> level
            x = ql[level][pl.ds(i * n * heads, n * heads), :].reshape(n, heads, width) * 0.5**level
            extra = x if extra is None else x + repeat_rows(extra, n // extra.shape[0])
        x = q32[pl.ds(i * CHUNK * heads, CHUNK * heads), :].reshape(CHUNK, heads, width)
        if extra is not None:
            x = x + repeat_rows(extra, 2)
        dq_ref[pl.ds(i * CHUNK, CHUNK)] = x.astype(BF16)
        return carry

    if levels > 5:
        total_q = jnp.zeros((CHUNK, heads, width), F32)
        for level in range(5, levels):
            x = ql[level][...].reshape(CHUNK, heads, width)
            for _ in range(level - 4):
                x = pair_sum(x)
            total_q = total_q + repeat_rows(x * 0.5**level, 1 << (level - 4))
        high[0] = total_q
    lax.fori_loop(0, chunks, finish_q, 0)

    first_back.wait_recv()
    for level in wide:
        remote_copy(
            back[level], back[level], sem_back_out.at[0], sem_back_in.at[level], sibling
        ).wait_recv()

    if levels > 5:
        for which in range(2):
            total_k = jnp.zeros((CHUNK, heads, width), F32)
            for level in range(5, levels):
                x = back[level][0, which].astype(F32)
                for j in range(1, back[level].shape[0]):
                    x = x + back[level][j, which].astype(F32)
                total_k = total_k + repeat_rows(x * 0.5**level, 1 << (level - 4))
            high[1 + which] = total_k

    def finish_kv(i, carry):
        for which, (near, out) in enumerate(((k32, dk_ref), (v32, dv_ref))):
            extra = high[1 + which, pl.ds(i, 1)] if levels > 5 else None
            for level in reversed(low):
                n = CHUNK >> level
                x = back[level][0, which, pl.ds(i * n, n)].astype(F32)
                for j in range(1, back[level].shape[0]):
                    x = x + back[level][j, which, pl.ds(i * n, n)].astype(F32)
                x = x * 0.5**level
                extra = x if extra is None else x + repeat_rows(extra, n // extra.shape[0])
            x = near[pl.ds(i * CHUNK * heads, CHUNK * heads), :].reshape(CHUNK, heads, width)
            if extra is not None:
                x = x + repeat_rows(extra, 2)
            out[pl.ds(i * CHUNK, CHUNK)] = x.astype(BF16)
        return carry

    lax.fori_loop(0, chunks, finish_kv, 0)

    for copy in sends + [first] + list(forwards.values()) + list(halves.values()):
        copy.wait_send()
    for copy in [first_back] + returns:
        copy.wait_send()


def on_device(query_rows, key_rows, value_rows, out_grad):
    rows, heads, width = query_rows.shape
    devices = lax.axis_size("seq")
    levels = (rows * devices // BLOCK).bit_length() - 1
    remote = range(1, levels)
    wide = range(2, levels)
    copies = 1 + sum(1 << (level - 2) for level in wide)
    half = BLOCK // 2

    def kept(level):
        return max(rows >> level, CHUNK)

    flat = (rows * heads, width)
    dma = pltpu.SemaphoreType.DMA
    scratch = [pltpu.VMEM(flat, F32) for _ in range(5)]
    scratch += [pltpu.VMEM((3, CHUNK, heads, width), F32) for _ in range(2)]
    scratch += [pltpu.VMEM((heads, rows, rows), F32), pltpu.VMEM((heads, rows, width), F32)]
    scratch += [pltpu.VMEM((heads, rows, 1), F32) for _ in range(4)]
    scratch += [dma((copies,)), dma((levels,)), dma((levels,)), dma((levels,))]
    scratch += [dma((levels,)), dma((levels,)), dma((copies,)), dma((levels,))]
    scratch += [pltpu.VMEM((kept(level) * heads, width), F32) for level in remote]
    scratch += [pltpu.VMEM((2, rows >> level, heads, width), BF16) for level in remote]
    scratch += [
        pltpu.VMEM((1, 2, BLOCK, heads, width) if level == 1 else (2, 2, half, heads, width), BF16)
        for level in remote
    ]
    scratch += [pltpu.VMEM((2, BLOCK * heads, width), F32) for level in remote]
    scratch += [
        pltpu.VMEM((2, BLOCK if level == 1 else half, heads, width), BF16) for level in remote
    ]
    for _ in range(2):
        scratch += [
            pltpu.VMEM((2, CHUNK if level == 1 else half, heads, width), BF16) for level in remote
        ]
    scratch += [
        pltpu.VMEM((max(1 << level >> 2, 1), 2, rows >> level, heads, width), BF16)
        for level in remote
    ]
    vmem = pl.BlockSpec(memory_space=pltpu.VMEM)
    out = jax.ShapeDtypeStruct(query_rows.shape, BF16)
    return pl.pallas_call(
        partial(kernel, levels, heads, width, rows),
        out_shape=(out, out, out, out),
        in_specs=[vmem] * 4,
        out_specs=(vmem,) * 4,
        scratch_shapes=scratch,
        compiler_params=pltpu.CompilerParams(
            collective_id=0, has_side_effects=True, vmem_limit_bytes=58 << 20
        ),
    )(query_rows, key_rows, value_rows, out_grad)


def solution(mesh):
    spec = P(("groups", "seq"), None, None)
    return jax.shard_map(
        on_device,
        mesh=mesh,
        in_specs=(spec,) * 4,
        out_specs=(spec,) * 4,
        check_vma=False,
    )
```

time: 219 us -> 64.5 us (0.29); the launches traced: 216 us -> 64.2 us
  local copies, waits for them, and re-layouts: 71 us -> 5.18 us
  other arithmetic: 61.8 us -> 0 us
  Pallas kernels: 0 us -> 58.4 us
  matrix products: 34.8 us -> 0 us
  waiting for transfers between devices: 31.8 us -> 0 us
  starting transfers between devices: 15.1 us -> 0 us
    pallas_call x0 -> x1, Pallas kernels: none -> 58.4 us  [on_device(): pl.pallas_call(partial(kernel, levels, heads, width, rows), out_shape=(ou...]
    dot_general x38 -> x0, matrix products: 34.8 us -> none  [the longest x18 19 us: block_term(): jnp.einsum('hbqk,hbkd->hbqd', keep_round(weights), value_blocks, precisio...]
    ppermute x20 -> x0, waiting for transfers between devices: 31.8 us -> none  [partner_2(): lax.ppermute(array, axis, [(i, i ^ 1 << stride) for i in range(lax.axis_s...]
    convert_element_type x24 -> x0, other arithmetic: 20.3 us -> none  [the longest x20 11.2 us: keep_round(): lowered = lax.optimization_barrier(frozen.astype(jnp.bfloat16))]
    ppermute x20 -> x0, starting transfers between devices: 15.1 us -> none  [partner_2(): lax.ppermute(array, axis, [(i, i ^ 1 << stride) for i in range(lax.axis_s...]
    reduce_sum x21 -> x0, other arithmetic: 14.1 us -> none  [the longest x8 10.6 us: upsample(): return tuple((jnp.repeat(entry, 2, axis=1) for entry in summary))]
    unnamed x242 -> x10, local copies, waits for them, and re-layouts: 14.6 us -> 5.18 us
    reshape x13 -> x0, local copies, waits for them, and re-layouts: 8.37 us -> none  [the longest x8 8.08 us: upsample(): return tuple((jnp.repeat(entry, 2, axis=1) for entry in summary))]
  transfers between devices with their start and end apart: 20 -> 0, of which waited for: 4 -> 0; matrix products, arithmetic and copies ran while one was open for 33% -> 0% of each run, Pallas kernels for 0% -> 0%
where the time goes in v1:
time: 64.5 us; the launch traced here: 64.2 us
  Pallas kernels  58.4 us (91%)
  local copies, waits for them, and re-layouts  5.18 us (8%)
  between operations  0.65 us (1%)
    pallas_call x1, Pallas kernels, on_device(): pl.pallas_call(partial(kernel, levels, heads, width, rows), out_shape=(ou...  58.4 us
    unnamed x10, local copies, waits for them, and re-layouts  5.18 us

profile of v1, /device:TPU:0, one launch (start us, length us, event | category | flops | bytes accessed | tf_op | source)
XLA Modules:
  0.0 64.2 jit_solution(3603039943490315766)
XLA Ops:
  0.6 58.4 %shard_map.75 = (bf16[256,8,128]{2,1,0:T(8,128)(2,1)}, bf16[256,8,128]{2,1,0:T(8,128)(2,1)}, bf16[256,8,128]{2,1,0:T(8,128)(2,1)}, bf16[256,8,128]{2,1,0:T(8,128)(2,1)}) custom-call(bf16[256,8,128]{2,1,0:T(8,128)(2,1)} %refs_0_.1, bf16[256,8,128]{2,1,0:T(8,128)(2,1)} %refs_1_.1, bf16[256,8,128]{2,1,0:T(8,128)(2,1)} %refs_2_.1, bf16[256,8,128]{2,1,0:T(8,128)(2,1)} %refs_3_.1), custom_call_target="tpu_custom_call" | custom-call | tf_op jit(solution)/shard_map/pallas_call | solution.py:439
  59.0 0.0 copy-start.2
  59.0 1.9 %copy.12 = bf16[256,8,128]{2,1,0:T(8,128)(2,1)} copy(bf16[256,8,128]{2,1,0:T(8,128)(2,1)} %get-tuple-element.8) | data formatting | bytes 1048576
  61.0 0.0 copy-done.2
  61.0 0.0 copy-start.1
  61.0 0.8 %copy.13 = bf16[256,8,128]{2,1,0:T(8,128)(2,1)} copy(bf16[256,8,128]{2,1,0:T(8,128)(2,1)S(1)} %copy-done.2) | data formatting | bytes 1048576
  61.8 0.4 copy-done.1
  62.2 0.0 copy-start
  62.2 0.8 %copy.14 = bf16[256,8,128]{2,1,0:T(8,128)(2,1)} copy(bf16[256,8,128]{2,1,0:T(8,128)(2,1)S(1)} %copy-done.1) | data formatting | bytes 1048576
  63.0 0.4 copy-done
  63.4 0.8 %copy.15 = bf16[256,8,128]{2,1,0:T(8,128)(2,1)} copy(bf16[256,8,128]{2,1,0:T(8,128)(2,1)S(1)} %copy-done) | data formatting | bytes 1048576
Async XLA Ops:
  59.0 1.9 %copy-start.2 = (bf16[256,8,128]{2,1,0:T(8,128)(2,1)S(1)}, bf16[256,8,128]{2,1,0:T(8,128)(2,1)}, u32[]{:S(2)}) copy-start(bf16[256,8,128]{2,1,0:T(8,128)(2,1)} %get-tuple-element.9) | copy-start | bytes 1572868
  61.0 1.2 %copy-start.1 = (bf16[256,8,128]{2,1,0:T(8,128)(2,1)S(1)}, bf16[256,8,128]{2,1,0:T(8,128)(2,1)}, u32[]{:S(2)}) copy-start(bf16[256,8,128]{2,1,0:T(8,128)(2,1)} %get-tuple-element.10) | copy-start | bytes 1572868
  62.2 1.2 %copy-start = (bf16[256,8,128]{2,1,0:T(8,128)(2,1)S(1)}, bf16[256,8,128]{2,1,0:T(8,128)(2,1)}, u32[]{:S(2)}) copy-start(bf16[256,8,128]{2,1,0:T(8,128)(2,1)} %get-tuple-element.11) | copy-start | bytes 1572868

commit v2 on v1

--- a/solution.py
+++ b/solution.py
@@ -63,9 +63,8 @@
     (sem_half_out, sem_half_in, sem_back_out, sem_back_in) = refs[25:29]
     per = levels - 1
     cut = 29
-    groups = [dict(zip(range(1, levels), refs[cut + i * per : cut + (i + 1) * per])) for i in range(7)]
-    ql, own, got, kv32, give, gain, total = groups
-    back = dict(zip(range(1, levels), refs[cut + 7 * per : cut + 8 * per]))
+    groups = [dict(zip(range(1, levels), refs[cut + i * per : cut + (i + 1) * per])) for i in range(14)]
+    ql, own, got, kv32, give, gain, total, back, pf, mf, lf, numf, gf, df = groups
     factor = width ** (-0.5)
     remote = list(range(1, levels))
     wide = [level for level in remote if level >= 2]
@@ -156,30 +155,42 @@
             lowered = repeat_rows((x * 0.5**level).astype(BF16).astype(F32), 1 << (level - 4))
             ql[level][...] = lowered.reshape(CHUNK * heads, width)
 
-    def near_forward(h, carry):
-        q = load_rows(q32, h, heads, 0).astype(BF16)
-        k = k32[pl.ds(h, rows, stride=heads), :].astype(BF16)
-        v = v32[pl.ds(h, rows, stride=heads), :].astype(BF16)
-        s = dot_nt(q, k) * factor
-        m = jnp.max(s, axis=1, keepdims=True)
-        p = jnp.exp(s - m)
-        p0[h] = p
-        m0[h] = m
-        l0[h] = jnp.sum(p, axis=1, keepdims=True)
-        num0[h] = dot_nn(p.astype(BF16), v)
-        return carry
-
-    lax.fori_loop(0, heads, near_forward, 0)
-
-    forwards = {}
-    for level in sorted(wide, reverse=True):
-        mine = got[level].at[core]
-        remote_copy(mine, mine, sem_out.at[0], sem_in.at[level], sibling).wait_recv()
-        forwards[level] = remote_copy(
-            mine, mine, sem_fwd_out.at[level], sem_fwd_in.at[level], sibling
-        )
-        forwards[level].start()
-    first.wait_recv()
+    def in_groups(count, body):
+        def step(i, carry):
+            body([i * count + j for j in range(count)])
+            return carry
+
+        lax.fori_loop(0, heads // count, step, 0)
+
+    def near_forward(hs):
+        q = [load_rows(q32, h, heads, 0).astype(BF16) for h in hs]
+        k = [k32[pl.ds(h, rows, stride=heads), :].astype(BF16) for h in hs]
+        v = [v32[pl.ds(h, rows, stride=heads), :].astype(BF16) for h in hs]
+        s = [dot_nt(x, y) * factor for x, y in zip(q, k)]
+        m = [jnp.max(x, axis=1, keepdims=True) for x in s]
+        p = [jnp.exp(x - y) for x, y in zip(s, m)]
+        num = [dot_nn(x.astype(BF16), y) for x, y in zip(p, v)]
+        for h, x, y, z in zip(hs, p, m, num):
+            p0[h] = x
+            m0[h] = y
+            l0[h] = jnp.sum(x, axis=1, keepdims=True)
+            num0[h] = z
+
+    def far_forward(level, hs):
+        q = [load_rows(ql[level], h, heads, level).astype(BF16) for h in hs]
+        k = [kv32[level][0, pl.ds(h, BLOCK, stride=heads), :].astype(BF16) for h in hs]
+        v = [kv32[level][1, pl.ds(h, BLOCK, stride=heads), :].astype(BF16) for h in hs]
+        s = [dot_nt(x, y) * factor for x, y in zip(q, k)]
+        m = [jnp.max(x, axis=1, keepdims=True) for x in s]
+        p = [jnp.exp(x - y) for x, y in zip(s, m)]
+        num = [dot_nn(x.astype(BF16), y) for x, y in zip(p, v)]
+        for h, x, y, z in zip(hs, p, m, num):
+            pf[level][h] = x
+            mf[level][h] = y
+            lf[level][h] = jnp.sum(x, axis=1, keepdims=True)
+            numf[level][h] = z
+
+    in_groups(2, near_forward)
 
     def widen(level):
         parts = got[level].shape[0]
@@ -197,75 +208,102 @@
 
         lax.fori_loop(0, 8, body, 0)
 
-    widen(1)
-    for level in sorted(wide, reverse=True):
+    def take(level):
         other = got[level].at[1 - core]
         remote_copy(other, other, sem_fwd_out.at[level], sem_fwd_in.at[level], sibling).wait_recv()
         widen(level)
-
-    def far(h, carry):
-        m_all = den = num = None
-        kept = {}
-        for level in reversed(remote):
-            q = load_rows(ql[level], h, heads, level).astype(BF16)
-            k = kv32[level][0, pl.ds(h, BLOCK, stride=heads), :].astype(BF16)
-            v = kv32[level][1, pl.ds(h, BLOCK, stride=heads), :].astype(BF16)
-            s = dot_nt(q, k) * factor
-            m = jnp.max(s, axis=1, keepdims=True)
-            p = jnp.exp(s - m)
-            pb = p.astype(BF16)
-            weight = float(1 << level)
-            den_l = jnp.sum(p, axis=1, keepdims=True)
-            num_l = dot_nn(pb, v)
-            if m_all is None:
-                scale_a, scale_b = None, jnp.full(m.shape, weight, F32)
-                m_all, den, num = m, den_l * weight, num_l * weight
-            else:
-                if m_all.shape[0] < m.shape[0]:
-                    m_all, den, num = (jnp.concatenate([x, x], 0) for x in (m_all, den, num))
-                top = jnp.maximum(m_all, m)
-                scale_a = jnp.exp(m_all - top)
-                scale_b = jnp.exp(m - top) * weight
-                m_all = top
-                den = scale_a * den + scale_b * den_l
-                num = scale_a * num + scale_b * num_l
-            kept[level] = (q, k, v, p, pb, scale_a, scale_b)
-        m = m0[h]
-        m_all, den, num = (jnp.concatenate([x, x], 0) for x in (m_all, den, num))
-        top = jnp.maximum(m_all, m)
-        scale_a = jnp.exp(m_all - top)
-        scale_b = jnp.exp(m - top)
-        den = scale_a * den + scale_b * l0[h]
-        num = scale_a * num + scale_b * num0[h]
-        inverse = 1.0 / den
-        att = num * inverse
-        store_rows(att32, h, heads, 0, att)
-        g = load_rows(g32, h, heads, 0)
-        d = jnp.sum(g * att, axis=1, keepdims=True)
-        c0[h] = scale_b * inverse
-        d0[h] = d
-        scale = scale_a * inverse
-        up, up_d = g * scale, d * scale
-        for level in remote:
-            q, k, v, p, pb, scale_a, scale_b = kept[level]
-            if up.shape[0] > q.shape[0]:
-                n = q.shape[0]
-                up, up_d = up[:n] + up[n:], up_d[:n] + up_d[n:]
-            gb = (up * scale_b).astype(BF16)
-            ds = (p * (dot_nt(gb, v) - up_d * scale_b) * factor).astype(BF16)
-            store_rows(ql[level], h, heads, level, dot_nn(ds, k))
-            kv32[level][0, pl.ds(h, BLOCK, stride=heads), :] = dot_tn(ds, q)
-            kv32[level][1, pl.ds(h, BLOCK, stride=heads), :] = dot_tn(pb, gb)
-            if scale_a is not None:
-                up, up_d = up * scale_a, up_d * scale_a
-        return carry
-
-    lax.fori_loop(0, heads, far, 0)
+        in_groups(4, partial(far_forward, level))
+
+    first.wait_recv()
+    widen(1)
+    in_groups(4, partial(far_forward, 1))
+
+    forwards = {}
+    order = sorted(wide, reverse=True)
+    for step, level in enumerate(order):
+        mine = got[level].at[core]
+        remote_copy(mine, mine, sem_out.at[0], sem_in.at[level], sibling).wait_recv()
+        forwards[level] = remote_copy(
+            mine, mine, sem_fwd_out.at[level], sem_fwd_in.at[level], sibling
+        )
+        forwards[level].start()
+        if step:
+            take(order[step - 1])
+    if order:
+        take(order[-1])
+
+    def merge(hs):
+        for h in hs:
+            state = None
+            scales = {}
+            for level in reversed(range(levels)):
+                if level:
+                    m, den_l, num_l = mf[level][h], lf[level][h], numf[level][h]
+                else:
+                    m, den_l, num_l = m0[h], l0[h], num0[h]
+                weight = float(1 << level)
+                if state is None:
+                    scale_a, scale_b = None, jnp.full(m.shape, weight, F32)
+                    state = (m, den_l * weight, num_l * weight)
+                else:
+                    if state[0].shape[0] < m.shape[0]:
+                        state = tuple(jnp.concatenate([x, x], 0) for x in state)
+                    top = jnp.maximum(state[0], m)
+                    scale_a = jnp.exp(state[0] - top)
+                    scale_b = jnp.exp(m - top) * weight
+                    state = (
+                        top,
+                        scale_a * state[1] + scale_b * den_l,
+                        scale_a * state[2] + scale_b * num_l,
+                    )
+                scales[level] = (scale_a, scale_b)
+            inverse = 1.0 / state[1]
+            att = state[2] * inverse
+            store_rows(att32, h, heads, 0, att)
+            g = load_rows(g32, h, heads, 0)
+            d = jnp.sum(g * att, axis=1, keepdims=True)
+            c0[h] = scales[0][1] * inverse
+            d0[h] = d
+            if levels == 1:
+                continue
+            scale = scales[0][0] * inverse
+            up, up_d = g * scale, d * scale
+            for level in remote:
+                scale_a, scale_b = scales[level]
+                if up.shape[0] > scale_b.shape[0]:
+                    n = scale_b.shape[0]
+                    up, up_d = up[:n] + up[n:], up_d[:n] + up_d[n:]
+                gf[level][h] = (up * scale_b).astype(BF16)
+                df[level][h] = up_d * scale_b
+                if scale_a is not None:
+                    up, up_d = up * scale_a, up_d * scale_a
+
+    in_groups(2, merge)
+
+    def far_backward(level, hs):
+        q = [load_rows(ql[level], h, heads, level).astype(BF16) for h in hs]
+        k = [kv32[level][0, pl.ds(h, BLOCK, stride=heads), :].astype(BF16) for h in hs]
+        v = [kv32[level][1, pl.ds(h, BLOCK, stride=heads), :].astype(BF16) for h in hs]
+        p = [pf[level][h] for h in hs]
+        g = [gf[level][h] for h in hs]
+        d = [df[level][h] for h in hs]
+        dp = [dot_nt(x, y) for x, y in zip(g, v)]
+        ds = [(x * (y - z) * factor).astype(BF16) for x, y, z in zip(p, dp, d)]
+        dv = [dot_tn(x.astype(BF16), y) for x, y in zip(p, g)]
+        dq = [dot_nn(x, y) for x, y in zip(ds, k)]
+        dk = [dot_tn(x, y) for x, y in zip(ds, q)]
+        for h, x, y, z in zip(hs, dq, dk, dv):
+            store_rows(ql[level], h, heads, level, x)
+            kv32[level][0, pl.ds(h, BLOCK, stride=heads), :] = y
+            kv32[level][1, pl.ds(h, BLOCK, stride=heads), :] = z
 
     halves = {}
-    for level in sorted(wide, reverse=True):
-
-        def narrow(i, carry, level=level):
+    returns = []
+
+    def leave(level):
+        in_groups(4, partial(far_backward, level))
+
+        def narrow(i, carry):
             n = half // 4
             for which in range(2):
                 x = kv32[level][which, pl.ds(((1 - core) * half + i * n) * heads, n * heads), :]
@@ -277,6 +315,34 @@
             give[level], gain[level], sem_half_out.at[level], sem_half_in.at[level], sibling
         )
         halves[level].start()
+
+    def pass_on(level):
+        halves[level].wait_recv()
+
+        def add(i, carry):
+            n = half // 4
+            for which in range(2):
+                x = kv32[level][which, pl.ds((core * half + i * n) * heads, n * heads), :]
+                y = gain[level][which, pl.ds(i * n, n)].astype(F32)
+                total[level][which, pl.ds(i * n, n)] = (x.reshape(n, heads, width) + y).astype(BF16)
+            return carry
+
+        lax.fori_loop(0, 4, add, 0)
+        n = rows >> level
+        for j, peer in enumerate(partners(level)):
+            returns.append(
+                remote_copy(
+                    total[level].at[:, pl.ds(j * n, n)], back[level].at[place(level)],
+                    sem_back_out.at[len(returns)], sem_back_in.at[level], peer,
+                )
+            )
+            returns[-1].start()
+
+    for step, level in enumerate(wide):
+        leave(level)
+        if step:
+            pass_on(wide[step - 1])
+    in_groups(4, partial(far_backward, 1))
 
     def narrow_first(i, carry):
         n = BLOCK // 8
@@ -285,50 +351,31 @@
             give[1][which, pl.ds(i * n, n)] = x.reshape(n, heads, width).astype(BF16)
         return carry
 
+    if wide:
+        pass_on(wide[-1])
     lax.fori_loop(0, 8, narrow_first, 0)
     first_back = remote_copy(
         give[1], back[1].at[0], sem_half_out.at[1], sem_back_in.at[1], sibling
     )
     first_back.start()
 
-    returns = []
-    slot = 0
-    for level in sorted(wide, reverse=True):
-        halves[level].wait_recv()
-
-        def add(i, carry, level=level):
-            n = half // 4
-            for which in range(2):
-                x = kv32[level][which, pl.ds((core * half + i * n) * heads, n * heads), :]
-                y = gain[level][which, pl.ds(i * n, n)].astype(F32)
-                total[level][which, pl.ds(i * n, n)] = (x.reshape(n, heads, width) + y).astype(BF16)
-            return carry
-
-        lax.fori_loop(0, 4, add, 0)
-        n = rows >> level
-        for j, peer in enumerate(partners(level)):
-            returns.append(
-                remote_copy(
-                    total[level].at[:, pl.ds(j * n, n)], back[level].at[place(level)],
-                    sem_back_out.at[slot], sem_back_in.at[level], peer,
-                )
-            )
-            returns[-1].start()
-            slot += 1
-
-    def near_backward(h, carry):
-        q = load_rows(q32, h, heads, 0).astype(BF16)
-        g = load_rows(g32, h, heads, 0).astype(BF16)
-        k = k32[pl.ds(h, rows, stride=heads), :].astype(BF16)
-        v = v32[pl.ds(h, rows, stride=heads), :].astype(BF16)
-        p = p0[h] * c0[h]
-        ds = (p * (dot_nt(g, v) - d0[h]) * factor).astype(BF16)
-        store_rows(q32, h, heads, 0, dot_nn(ds, k))
-        k32[pl.ds(h, rows, stride=heads), :] = dot_tn(ds, q)
-        v32[pl.ds(h, rows, stride=heads), :] = dot_tn(p.astype(BF16), g)
-        return carry
-
-    lax.fori_loop(0, heads, near_backward, 0)
+    def near_backward(hs):
+        q = [load_rows(q32, h, heads, 0).astype(BF16) for h in hs]
+        g = [load_rows(g32, h, heads, 0).astype(BF16) for h in hs]
+        k = [k32[pl.ds(h, rows, stride=heads), :].astype(BF16) for h in hs]
+        v = [v32[pl.ds(h, rows, stride=heads), :].astype(BF16) for h in hs]
+        p = [p0[h] * c0[h] for h in hs]
+        dp = [dot_nt(x, y) for x, y in zip(g, v)]
+        ds = [(x * (y - d0[h]) * factor).astype(BF16) for x, y, h in zip(p, dp, hs)]
+        dv = [dot_tn(x.astype(BF16), y) for x, y in zip(p, g)]
+        dq = [dot_nn(x, y) for x, y in zip(ds, k)]
+        dk = [dot_tn(x, y) for x, y in zip(ds, q)]
+        for h, x, y, z in zip(hs, dq, dk, dv):
+            store_rows(q32, h, heads, 0, x)
+            k32[pl.ds(h, rows, stride=heads), :] = y
+            v32[pl.ds(h, rows, stride=heads), :] = z
+
+    in_groups(2, near_backward)
 
     low = range(1, min(levels, 5))
 
@@ -394,6 +441,14 @@
         copy.wait_send()
     for copy in [first_back] + returns:
         copy.wait_send()
+
+
+def hand_over(*refs):
+    copies = [pltpu.make_async_copy(refs[i], refs[4 + i], refs[8].at[i]) for i in range(4)]
+    for copy in copies:
+        copy.start()
+    for copy in copies:
+        copy.wait()
 
 
 def on_device(query_rows, key_rows, value_rows, out_grad):
@@ -434,9 +489,11 @@
         pltpu.VMEM((max(1 << level >> 2, 1), 2, rows >> level, heads, width), BF16)
         for level in remote
     ]
+    for depth, kind in ((BLOCK, F32), (1, F32), (1, F32), (width, F32), (width, BF16), (1, F32)):
+        scratch += [pltpu.VMEM((heads, kept(level), depth), kind) for level in remote]
     vmem = pl.BlockSpec(memory_space=pltpu.VMEM)
     out = jax.ShapeDtypeStruct(query_rows.shape, BF16)
-    return pl.pallas_call(
+    made = pl.pallas_call(
         partial(kernel, levels, heads, width, rows),
         out_shape=(out, out, out, out),
         in_specs=[vmem] * 4,
@@ -446,6 +503,14 @@
             collective_id=0, has_side_effects=True, vmem_limit_bytes=58 << 20
         ),
     )(query_rows, key_rows, value_rows, out_grad)
+    whole = pl.BlockSpec(memory_space=pl.ANY)
+    return pl.pallas_call(
+        hand_over,
+        out_shape=(out, out, out, out),
+        in_specs=[whole] * 4,
+        out_specs=(whole,) * 4,
+        scratch_shapes=[dma((4,))],
+    )(*made)
 
 
 def solution(mesh):

time: 64.5 us -> 112 us (1.74); the launches traced: 64.2 us -> 110 us
  Pallas kernels: 58.4 us -> 110 us
  local copies, waits for them, and re-layouts: 5.18 us -> 0 us
    pallas_call x0 -> x1, Pallas kernels: none -> 64.7 us  [on_device(): pl.pallas_call(hand_over, out_shape=(out, out, out, out), in_specs=[whole...]
    pallas_call x1, Pallas kernels: 58.4 us -> 45.2 us  [on_device(): pl.pallas_call(partial(kernel, levels, heads, width, rows), out_shape=(ou...]
    unnamed x10 -> x0, local copies, waits for them, and re-layouts: 5.18 us -> none
where the time goes in v2:
time: 112 us; the launch traced here: 110 us
  Pallas kernels  110 us (98%)
    pallas_call x1, Pallas kernels, on_device(): pl.pallas_call(hand_over, out_shape=(out, out, out, out), in_specs=[whole...  64.7 us
    pallas_call x1, Pallas kernels, on_device(): pl.pallas_call(partial(kernel, levels, heads, width, rows), out_shape=(ou...  45.2 us

profile of v2, /device:TPU:0, one launch (start us, length us, event | category | flops | bytes accessed | tf_op | source)
XLA Modules:
  0.0 110.5 jit_solution(14287387583462831634)
XLA Ops:
  0.6 45.2 %shard_map.75 = (bf16[256,8,128]{2,1,0:T(8,128)(2,1)}, bf16[256,8,128]{2,1,0:T(8,128)(2,1)}, bf16[256,8,128]{2,1,0:T(8,128)(2,1)}, bf16[256,8,128]{2,1,0:T(8,128)(2,1)}) custom-call(bf16[256,8,128]{2,1,0:T(8,128)(2,1)} %refs_0_.1, bf16[256,8,128]{2,1,0:T(8,128)(2,1)} %refs_1_.1, bf16[256,8,128]{2,1,0:T(8,128)(2,1)} %refs_2_.1, bf16[256,8,128]{2,1,0:T(8,128)(2,1)} %refs_3_.1), custom_call_target="tpu_custom_call" | custom-call | tf_op jit(solution)/shard_map/pallas_call | solution.py:496
  45.8 64.7 %shard_map.76 = (bf16[256,8,128]{2,1,0:T(8,128)(2,1)}, bf16[256,8,128]{2,1,0:T(8,128)(2,1)}, bf16[256,8,128]{2,1,0:T(8,128)(2,1)}, bf16[256,8,128]{2,1,0:T(8,128)(2,1)}) custom-call(bf16[256,8,128]{2,1,0:T(8,128)(2,1)} %get-tuple-element.8.refs_0_, bf16[256,8,128]{2,1,0:T(8,128)(2,1)} %get-tuple-element.9.refs_1_, ...), custom_call_target="tpu_custom_call" | custom-call | tf_op jit(solution)/shard_map/pallas_call | solution.py:507

commit v3 on v2

--- a/solution.py
+++ b/solution.py
@@ -118,7 +118,7 @@
     pl.semaphore_wait(barrier, len(peers))
     sends = []
     slot = 0
-    for level in sorted(wide, reverse=True):
+    for level in wide:
         n = rows >> level
         at = place(level) * n
         for peer in partners(level):
@@ -212,14 +212,14 @@
         other = got[level].at[1 - core]
         remote_copy(other, other, sem_fwd_out.at[level], sem_fwd_in.at[level], sibling).wait_recv()
         widen(level)
-        in_groups(4, partial(far_forward, level))
+        in_groups(8, partial(far_forward, level))
 
     first.wait_recv()
     widen(1)
-    in_groups(4, partial(far_forward, 1))
+    in_groups(8, partial(far_forward, 1))
 
     forwards = {}
-    order = sorted(wide, reverse=True)
+    order = wide
     for step, level in enumerate(order):
         mine = got[level].at[core]
         remote_copy(mine, mine, sem_out.at[0], sem_in.at[level], sibling).wait_recv()
@@ -301,7 +301,7 @@
     returns = []
 
     def leave(level):
-        in_groups(4, partial(far_backward, level))
+        in_groups(8, partial(far_backward, level))
 
         def narrow(i, carry):
             n = half // 4
@@ -342,7 +342,7 @@
         leave(level)
         if step:
             pass_on(wide[step - 1])
-    in_groups(4, partial(far_backward, 1))
+    in_groups(8, partial(far_backward, 1))
 
     def narrow_first(i, carry):
         n = BLOCK // 8
@@ -444,10 +444,16 @@
 
 
 def hand_over(*refs):
-    copies = [pltpu.make_async_copy(refs[i], refs[4 + i], refs[8].at[i]) for i in range(4)]
-    for copy in copies:
+    given, made, held = refs[:4], refs[4:8], refs[8:12]
+    arrive, leave = refs[12:]
+    inward = [pltpu.make_async_copy(given[i], held[i], arrive.at[i]) for i in range(4)]
+    outward = [pltpu.make_async_copy(held[i], made[i], leave.at[i]) for i in range(4)]
+    for copy in inward:
         copy.start()
-    for copy in copies:
+    for i in range(4):
+        inward[i].wait()
+        outward[i].start()
+    for copy in outward:
         copy.wait()
 
 
@@ -509,7 +515,7 @@
         out_shape=(out, out, out, out),
         in_specs=[whole] * 4,
         out_specs=(whole,) * 4,
-        scratch_shapes=[dma((4,))],
+        scratch_shapes=[pltpu.VMEM(query_rows.shape, BF16) for _ in range(4)] + [dma((4,)), dma((4,))],
     )(*made)
 
 

time: 112 us -> 47.3 us (0.42); the launches traced: 110 us -> 47.1 us
  Pallas kernels: 110 us -> 46.4 us
    pallas_call x1, Pallas kernels: 64.7 us -> 2.42 us  [on_device(): pl.pallas_call(hand_over, out_shape=(out, out, out, out), in_specs=[whole...]
    pallas_call x1, Pallas kernels: 45.2 us -> 44 us  [on_device(): pl.pallas_call(partial(kernel, levels, heads, width, rows), out_shape=(ou...]
where the time goes in v3:
time: 47.3 us; the launch traced here: 47.1 us
  Pallas kernels  46.4 us (98%)
  between operations  0.64 us (1%)
    pallas_call x1, Pallas kernels, on_device(): pl.pallas_call(partial(kernel, levels, heads, width, rows), out_shape=(ou...  44 us
    pallas_call x1, Pallas kernels, on_device(): pl.pallas_call(hand_over, out_shape=(out, out, out, out), in_specs=[whole...  2.42 us

profile of v3, /device:TPU:0, one launch (start us, length us, event | category | flops | bytes accessed | tf_op | source)
XLA Modules:
  0.0 47.1 jit_solution(7192511145853768231)
XLA Ops:
  0.6 44.0 %shard_map.75 = (bf16[256,8,128]{2,1,0:T(8,128)(2,1)}, bf16[256,8,128]{2,1,0:T(8,128)(2,1)}, bf16[256,8,128]{2,1,0:T(8,128)(2,1)}, bf16[256,8,128]{2,1,0:T(8,128)(2,1)}) custom-call(bf16[256,8,128]{2,1,0:T(8,128)(2,1)} %refs_0_.1, bf16[256,8,128]{2,1,0:T(8,128)(2,1)} %refs_1_.1, bf16[256,8,128]{2,1,0:T(8,128)(2,1)} %refs_2_.1, bf16[256,8,128]{2,1,0:T(8,128)(2,1)} %refs_3_.1), custom_call_target="tpu_custom_call" | custom-call | tf_op jit(solution)/shard_map/pallas_call | solution.py:502
  44.6 2.4 %shard_map.76 = (bf16[256,8,128]{2,1,0:T(8,128)(2,1)}, bf16[256,8,128]{2,1,0:T(8,128)(2,1)}, bf16[256,8,128]{2,1,0:T(8,128)(2,1)}, bf16[256,8,128]{2,1,0:T(8,128)(2,1)}) custom-call(bf16[256,8,128]{2,1,0:T(8,128)(2,1)} %get-tuple-element.8.refs_0_, bf16[256,8,128]{2,1,0:T(8,128)(2,1)} %get-tuple-element.9.refs_1_, ...), custom_call_target="tpu_custom_call" | custom-call | tf_op jit(solution)/shard_map/pallas_call | solution.py:513

commit v4 on v3

--- a/solution.py
+++ b/solution.py
@@ -58,6 +58,12 @@
 
 def kernel(levels, heads, width, rows, *refs):
     q_ref, k_ref, v_ref, g_ref, o_ref, dq_ref, dk_ref, dv_ref = refs[:8]
+    q_hbm, g_hbm, o_hbm, dq_hbm = q_ref, g_ref, o_ref, dq_ref
+    q_ref, g_ref, o_ref, dq_ref, sem_local = refs[-5:]
+    fetch_q = pltpu.make_async_copy(q_hbm, q_ref, sem_local.at[0])
+    fetch_g = pltpu.make_async_copy(g_hbm, g_ref, sem_local.at[1])
+    fetch_q.start()
+    fetch_g.start()
     (q32, k32, v32, g32, att32, tops, high, p0, num0, m0, l0, c0, d0) = refs[8:21]
     (sem_out, sem_in, sem_fwd_out, sem_fwd_in) = refs[21:25]
     (sem_half_out, sem_half_in, sem_back_out, sem_back_in) = refs[25:29]
@@ -147,6 +153,8 @@
         g32[pl.ds(i * CHUNK * heads, CHUNK * heads), :] = g.reshape(CHUNK * heads, width)
         return carry
 
+    fetch_q.wait()
+    fetch_g.wait()
     lax.fori_loop(0, chunks, prepare_q, 0)
     if levels > 5:
         x = tops[2]
@@ -278,7 +286,7 @@
                 if scale_a is not None:
                     up, up_d = up * scale_a, up_d * scale_a
 
-    in_groups(2, merge)
+    in_groups(4, merge)
 
     def far_backward(level, hs):
         q = [load_rows(ql[level], h, heads, level).astype(BF16) for h in hs]
@@ -402,6 +410,10 @@
             total_q = total_q + repeat_rows(x * 0.5**level, 1 << (level - 4))
         high[0] = total_q
     lax.fori_loop(0, chunks, finish_q, 0)
+    store_o = pltpu.make_async_copy(o_ref, o_hbm, sem_local.at[2])
+    store_q = pltpu.make_async_copy(dq_ref, dq_hbm, sem_local.at[3])
+    store_o.start()
+    store_q.start()
 
     first_back.wait_recv()
     for level in wide:
@@ -437,6 +449,8 @@
 
     lax.fori_loop(0, chunks, finish_kv, 0)
 
+    store_o.wait()
+    store_q.wait()
     for copy in sends + [first] + list(forwards.values()) + list(halves.values()):
         copy.wait_send()
     for copy in [first_back] + returns:
@@ -497,13 +511,15 @@
     ]
     for depth, kind in ((BLOCK, F32), (1, F32), (1, F32), (width, F32), (width, BF16), (1, F32)):
         scratch += [pltpu.VMEM((heads, kept(level), depth), kind) for level in remote]
+    scratch += [pltpu.VMEM(query_rows.shape, BF16) for _ in range(4)] + [dma((4,))]
     vmem = pl.BlockSpec(memory_space=pltpu.VMEM)
+    whole = pl.BlockSpec(memory_space=pl.ANY)
     out = jax.ShapeDtypeStruct(query_rows.shape, BF16)
     made = pl.pallas_call(
         partial(kernel, levels, heads, width, rows),
         out_shape=(out, out, out, out),
-        in_specs=[vmem] * 4,
-        out_specs=(vmem,) * 4,
+        in_specs=[whole, vmem, vmem, whole],
+        out_specs=(whole, whole, vmem, vmem),
         scratch_shapes=scratch,
         compiler_params=pltpu.CompilerParams(
             collective_id=0, has_side_effects=True, vmem_limit_bytes=58 << 20

time: 47.3 us -> 46.6 us (0.985)
  Pallas kernels: 46.4 us -> 45.7 us
    pallas_call x1, Pallas kernels: 44 us -> 43.2 us  [on_device(): pl.pallas_call(partial(kernel, levels, heads, width, rows), out_shape=(ou...]
where the time goes in v4:
time: 46.6 us; the launch traced here: 46.3 us
  Pallas kernels  45.7 us (98%)
  between operations  0.64 us (1%)
    pallas_call x1, Pallas kernels, on_device(): pl.pallas_call(partial(kernel, levels, heads, width, rows), out_shape=(ou...  43.2 us
    pallas_call x1, Pallas kernels, on_device(): pl.pallas_call(hand_over, out_shape=(out, out, out, out), in_specs=[whole...  2.42 us

profile of v4, /device:TPU:0, one launch (start us, length us, event | category | flops | bytes accessed | tf_op | source)
XLA Modules:
  0.0 46.3 jit_solution(18177770130273711976)
XLA Ops:
  0.6 43.2 %shard_map.75 = (bf16[256,8,128]{2,1,0:T(8,128)(2,1)}, bf16[256,8,128]{2,1,0:T(8,128)(2,1)}, bf16[256,8,128]{2,1,0:T(8,128)(2,1)}, bf16[256,8,128]{2,1,0:T(8,128)(2,1)}) custom-call(bf16[256,8,128]{2,1,0:T(8,128)(2,1)} %refs_0_.1, bf16[256,8,128]{2,1,0:T(8,128)(2,1)} %refs_1_.1, bf16[256,8,128]{2,1,0:T(8,128)(2,1)} %refs_2_.1, bf16[256,8,128]{2,1,0:T(8,128)(2,1)} %refs_3_.1), custom_call_target="tpu_custom_call" | custom-call | tf_op jit(solution)/shard_map/pallas_call | solution.py:518
  43.9 2.4 %shard_map.76 = (bf16[256,8,128]{2,1,0:T(8,128)(2,1)}, bf16[256,8,128]{2,1,0:T(8,128)(2,1)}, bf16[256,8,128]{2,1,0:T(8,128)(2,1)}, bf16[256,8,128]{2,1,0:T(8,128)(2,1)}) custom-call(bf16[256,8,128]{2,1,0:T(8,128)(2,1)} %get-tuple-element.8.refs_0_, bf16[256,8,128]{2,1,0:T(8,128)(2,1)} %get-tuple-element.9.refs_1_, ...), custom_call_target="tpu_custom_call" | custom-call | tf_op jit(solution)/shard_map/pallas_call | solution.py:529
